TPU v7x, 32 devices: a whole 2x2x4 slice. The times are simulated.
32 devices in a mesh: groups: 2 (over y), seq: 4 (over z), mp: 2 (over x), rep: 2 (over core).
Axes of the slice: x: 2, y: 2, z: 4, core: 2. Of those that a mesh axis runs over, the one named last changes fastest.
Arguments:
- tokens: bfloat16 [8192, 2240], P(('groups', 'seq', 'rep')), parts along dimension 0, may hold values from -8 to 8
- slot_image: int32 [32], P(('groups', 'seq', 'rep')), parts along dimension 0, may hold values from 0 to 5, as said below
- modulation: float32 [12, 3, 2240], P('groups'), parts along dimension 0, may hold values from -3 to 3
- w_qkv: bfloat16 [2240, 3, 1280], P('rep', None, 'mp'), may hold values from -0.125 to 0.125
- w_out: bfloat16 [1280, 2240], P('rep', 'mp'), may hold values from -0.15625 to 0.15625
Outputs:
- updated: bfloat16 [8192, 2240], P(('groups', 'seq', 'rep'), 'mp'), parts along dimension 0
There are 2 independent parts, one for each index of `groups`. A program takes and returns all parts, laid end to end along the dimension named above; an argument that names none is the same for every part. Nothing has to cross between parts.
Inputs may be any that keep to these rules, and one draw needn't show every extreme that they name: `slot_image`: every one of the 6 images owns one tile slot or more.
All inputs are finite; a program needn't handle non-finite values.
Results may differ from a plain program's by a relative error of at most 0.0036.
Values may be sent and summed in bfloat16 or wider, within the bound.
No kernel may reach another device: no remote copies, remote signals or barrier semaphores. Data moves between devices by JAX's collectives and lax.ppermute only.
A program may use at most 128 MiB of HBM per device.

v0:
```python
import jax
import jax.numpy as jnp
from jax import lax
from jax.sharding import PartitionSpec as P

D = 2240
HD = 32


def body(tokens, slot_image, modulation, w_qkv, w_out):
    hi = lax.Precision.HIGHEST
    tiles = slot_image.shape[0]
    rows = tokens.shape[0]
    tile_len = rows // tiles
    images = modulation.shape[0]
    width = w_qkv.shape[2]
    per_dev = width // HD
    picker = (slot_image[:, None] == jnp.arange(images, dtype=jnp.int32)[None, :]).astype(
        jnp.float32
    )
    per_tile = jnp.dot(picker, modulation.reshape(images, 3 * D), precision=hi).reshape(tiles, 3, D)
    xf = tokens.astype(jnp.float32).reshape(tiles, tile_len, D)
    mean = jnp.mean(xf, axis=2, keepdims=True)
    var = jnp.mean((xf - mean) ** 2, axis=2, keepdims=True)
    normed = (xf - mean) / jnp.sqrt(var + 1e-06)
    modulated = (normed * (1.0 + per_tile[:, None, 1, :]) + per_tile[:, None, 0, :]).astype(
        jnp.bfloat16
    )
    modulated = modulated.reshape(rows, D)
    qkv = jnp.einsum(
        "td,dcm->tcm",
        modulated,
        lax.all_gather(w_qkv, "rep", axis=0, tiled=True),
        preferred_element_type=jnp.float32,
    )
    qkv = qkv.reshape(tiles, tile_len, 3, per_dev, HD)
    query = jax.nn.relu(qkv[:, :, 0]).astype(jnp.bfloat16)
    keyf = jax.nn.relu(qkv[:, :, 1]).astype(jnp.bfloat16)
    value = qkv[:, :, 2].astype(jnp.bfloat16)
    tile_state = jnp.einsum("slhe,slhf->shef", keyf, value, preferred_element_type=jnp.float32)
    tile_ksum = jnp.sum(keyf.astype(jnp.float32), axis=1)
    state = jnp.einsum("si,shef->ihef", picker, tile_state, precision=hi)
    ksum = jnp.einsum("si,she->ihe", picker, tile_ksum, precision=hi)
    state, ksum = lax.psum((state, ksum), ("seq", "rep"))
    own_state = jnp.einsum("si,ihef->shef", picker, state, precision=hi)
    own_ksum = jnp.einsum("si,ihe->she", picker, ksum, precision=hi)
    query_wide = query.astype(jnp.float32)
    numer = jnp.einsum("slhe,shef->slhf", query_wide, own_state, precision=hi)
    denom = jnp.einsum("slhe,she->slh", query_wide, own_ksum, precision=hi) + 1e-06
    attn = (numer / denom[..., None]).astype(jnp.bfloat16).reshape(rows, per_dev * HD)
    out_full = lax.all_gather(w_out, "rep", axis=0, tiled=True)
    cols = out_full.shape[1]
    projected = jnp.dot(
        lax.all_gather(attn, "mp", axis=1, tiled=True), out_full, preferred_element_type=jnp.float32
    )
    offset = lax.axis_index("mp") * cols
    own_tokens = (
        lax.dynamic_slice_in_dim(tokens, offset, cols, 1)
        .astype(jnp.float32)
        .reshape(tiles, tile_len, cols)
    )
    gate = lax.dynamic_slice_in_dim(per_tile[:, 2, :], offset, cols, 1)
    updated = own_tokens + gate[:, None, :] * projected.reshape(tiles, tile_len, cols)
    return updated.astype(jnp.bfloat16).reshape(rows, cols)


def solution(mesh):
    return jax.shard_map(
        body,
        mesh=mesh,
        in_specs=(
            P(("groups", "seq", "rep"), None),
            P(("groups", "seq", "rep")),
            P("groups", None, None),
            P("rep", None, "mp"),
            P("rep", "mp"),
        ),
        out_specs=P(("groups", "seq", "rep"), "mp"),
        check_vma=False,
    )
```

profile of v0, /device:TPU:0, one launch (start us, length us, event | category | flops | bytes accessed | tf_op | source)
XLA Modules:
  0.0 175.1 jit_solution(10275999285317942195)
XLA Ops:
  6.5 0.7 all-gather.4.cloned.1.call-update
  8.1 0.4 copy.12
  8.5 2.7 %mul.34 = f32[2,256,2240]{1,0,2:T(2,128)S(1)} broadcast(f32[2,2240]{0,1:T(8,128)S(1)} %copy.12), dimensions={0,2} | broadcast | bytes 4605440 | tf_op jit(solution)/shard_map/mul | solution.py:26
  11.3 2.6 %copy.34 = f32[280,8,2,256]{3,1,2,0:T(8,128)} copy(f32[280,8,2,256]{3,2,1,0:T(2,128)S(1)} %bitcast.80) | data formatting | bytes 9175040
  13.8 0.4 copy.13
  14.2 2.7 %add.57 = f32[2,256,2240]{1,0,2:T(2,128)S(1)} broadcast(f32[2,2240]{0,1:T(8,128)S(1)} %copy.13), dimensions={0,2} | broadcast | bytes 4605440 | tf_op jit(solution)/shard_map/add | solution.py:26
  17.0 0.5 copy.35
  17.5 1.5 copy-done
  19.0 0.4 convert_reduce_fusion
  19.4 0.7 fusion.2
  20.1 3.0 %fusion.5 = bf16[512,2240]{0,1:T(8,128)(2,1)} fusion(f32[512,2240]{0,1:T(8,128)S(1)} %bitcast.79, f32[512,2240]{0,1:T(8,128)S(1)} %bitcast.78, bf16[512,2240]{0,1:T(8,128)(2,1)S(1)} %copy-done, f32[512]{0:T(512)S(1)} %add_sqrt_fusion, f32[512]{0:T(512)S(1)} %broadcast_multiply_fusion), kind=kLoop, calls=%fused_computation.7 | loop fusion | flops 6881280 | bytes 13766656 | tf_op jit(solution)/shard_map/convert_element_type | solution.py:26
  23.1 6.1 %dot_general.43 = bf16[2,256,2240]{1,0,2:T(2,128)(2,1)} reshape(bf16[512,2240]{0,1:T(8,128)(2,1)} %fusion.5) | data formatting | bytes 4587520 | tf_op jit(solution)/shard_map/td,dcm->tcm/dot_general | solution.py:30
  29.2 1.7 all-gather.4.cloned.1.call-done
  30.9 13.2 %copy.14 = bf16[3,640,2240]{2,1,0:T(8,128)(2,1)} copy(bf16[3,640,2240]{1,2,0:T(8,128)(2,1)} %bitcast.84) | data formatting | bytes 17203200 | tf_op jit(solution)/shard_map/td,dcm->tcm/dot_general | solution.py:30
  44.1 8.9 %fusion.10 = bf16[2,256,3,20,32]{1,4,3,2,0:T(8,128)(2,1)S(1)} fusion(bf16[3,20,32,2240,1]{3,2,1,0,4:T(8,128)(2,1)} %bitcast.83, bf16[2,256,2240,1,1]{1,0,2,4,3:T(2,128)(2,1)} %bitcast.88), kind=kOutput, calls=%fused_computation.13 | convolution fusion | flops 4404019200 | bytes 12861440 | tf_op jit(solution)/shard_map/td,dcm->tcm/dot_general | solution.py:30
  53.1 0.3 fusion.18
  53.4 1.9 %fusion.22 = f32[6,20,32,32]{3,0,2,1:T(8,128)S(1)} fusion(f32[2,20,32,32]{3,2,1,0:T(8,128)S(1)} %fusion.18, s32[2]{0:T(128)S(1)} %copy-done.3), kind=kOutput, calls=%fused_computation.30 | convolution fusion | flops 2949132 | bytes 655368 | tf_op jit(solution)/shard_map/si,shef->ihef/dot_general | solution.py:42
  55.4 1.7 copy.20
  57.2 0.7 all-gather.8.cloned.1.call-update
  57.9 1.3 convert_reduce_fusion.1
  59.6 31.6 %psum.15 = f32[6,20,32]{2,1,0:T(8,128)S(1)} all-reduce(f32[6,20,32]{2,1,0:T(8,128)S(1)} %copy.24), channel_id=1, replica_groups=mesh['groups'=2,'seq'=4,'mp'=2,'rep'=2] {'seq','rep'}, use_global_device_ids=true, to_apply=%region_4.5 | all-reduce | flops 3840 | bytes 30720 | tf_op jit(solution)/shard_map/psum | solution.py:44
  91.4 1.5 fusion.27
  92.9 30.4 %all-reduce.2.cloned.1.call-done = f32[6,20,32,32]{3,2,1,0:T(8,128)} async-done(((f32[6,20,32,32]{3,2,1,0:T(8,128)}), f32[6,20,32,32]{3,2,1,0:T(8,128)}) %all-reduce.2.cloned.1.call-update) | async-done | bytes 491536 | tf_op jit(solution)/shard_map/psum | solution.py:44
  123.3 3.9 %fusion.8 = f32[2,20,32,32]{3,0,2,1:T(2,128)S(1)} fusion(f32[6,20,32,32]{3,2,1,0:T(8,128)} %all-reduce.2.cloned.1.call-done, s32[2]{0:T(128)S(1)} %copy-done.3), kind=kOutput, calls=%fused_computation.11 | convolution fusion | flops 2949132 | bytes 655368 | tf_op jit(solution)/shard_map/si,ihef->shef/dot_general | solution.py:45
  127.2 1.9 %fusion.13 = bf16[2,256,20,32]{1,3,2,0:T(8,128)(2,1)S(1)} fusion(f32[2,20,32,32]{3,0,2,1:T(2,128)S(1)} %fusion.8, f32[2,256,20]{1,2,0:T(8,128)S(1)} %fusion.31, bf16[2,256,3,20,32]{1,4,3,2,0:T(8,128)(2,1)} %copy-done.2), kind=kOutput, calls=%fused_computation.17 | convolution fusion | flops 127467520 | bytes 1515520 | tf_op jit(solution)/shard_map/slhe,shef->slhf/dot_general | solution.py:48
  129.1 0.7 copy.16
  129.8 0.9 copy.36
  131.1 1.3 mul.31
  132.5 1.6 copy.33
  134.1 2.0 %all-gather.8.cloned.1.call-done = bf16[1280,1120]{0,1:T(8,128)(2,1)} async-done(((bf16[640,1120]{0,1:T(8,128)(2,1)}), bf16[1280,1120]{0,1:T(8,128)(2,1)}) %all-gather.8.cloned.1.call-update) | async-done | bytes 2867216 | tf_op jit(solution)/shard_map/all_gather | solution.py:51
  136.1 26.8 %all-gather.6.cloned.1.call-done = bf16[512,1280]{0,1:T(8,128)(2,1)} async-done(((bf16[512,640]{0,1:T(8,128)(2,1)}), bf16[512,1280]{0,1:T(8,128)(2,1)}) %all-gather.6.cloned.1.call-update) | async-done | bytes 1310736 | tf_op jit(solution)/shard_map/all_gather | solution.py:54
  162.9 5.6 %fusion.7 = bf16[512,1120]{0,1:T(8,128)(2,1)} fusion(f32[512,1120]{0,1:T(8,128)} %bitcast.87, bf16[1280,1120]{0,1:T(8,128)(2,1)} %all-gather.8.cloned.1.call-done, bf16[512,1280]{0,1:T(8,128)(2,1)} %all-gather.6.cloned.1.call-done, bf16[512,2240]{0,1:T(8,128)(2,1)S(1)} %copy-done, s32[]{:T(128)S(6)} %select_n.4), kind=kOutput, calls=%fused_computation.10 | convolution fusion | flops 1470300160 | bytes 8765444 | tf_op jit(solution)/shard_map/dot_general | solution.py:53
  (30 shorter events, 1.9 us)
Async XLA Ops:
  6.5 0.9 copy-start.1
  6.5 24.4 %all-gather.4.cloned.1.call-start = ((), (), s32[]{:S(2)}) async-start(), calls=%async_computation | async-start | bytes 12902400 | tf_op jit(solution)/shard_map/all_gather | solution.py:33
  6.5 1.3 copy-start.3
  7.3 116.1 %all-reduce.2.cloned.1.call-start = ((), (), s32[]{:S(2)}) async-start(), calls=%async_computation.1 | async-start | bytes 3932160 | tf_op jit(solution)/shard_map/psum | solution.py:44
  14.2 5.9 %slice-start = ((s8[4587520]{0:T(1024)(128)(4,1)}), s8[4194304]{0:T(1024)(128)(4,1)S(1)}, s32[]{:S(2)}) async-start(s8[4587520]{0:T(1024)(128)(4,1)} %bitcast.76), calls=%async_computation.4 | async-start | bytes 8388608
  17.0 2.1 %copy-start = (bf16[512,2240]{0,1:T(8,128)(2,1)S(1)}, bf16[512,2240]{0,1:T(8,128)(2,1)}, u32[]{:S(2)}) copy-start(bf16[512,2240]{0,1:T(8,128)(2,1)} %param.5) | copy-start | bytes 6881284
  17.0 3.1 %slice-start.1 = ((s8[4587520]{0:T(1024)(128)(4,1)}), s8[393216]{0:T(1024)(128)(4,1)S(1)}, s32[]{:S(2)}) async-start(s8[4587520]{0:T(1024)(128)(4,1)} %bitcast.76), calls=%async_computation.5 | async-start | bytes 786432
  53.1 2.3 %copy-start.2 = (bf16[2,256,3,20,32]{1,4,3,2,0:T(8,128)(2,1)}, bf16[2,256,3,20,32]{1,4,3,2,0:T(8,128)(2,1)S(1)}, u32[]{:S(2)}) copy-start(bf16[2,256,3,20,32]{1,4,3,2,0:T(8,128)(2,1)S(1)} %fusion.10) | copy-start | bytes 5898244
  57.1 79.0 %all-gather.8.cloned.1.call-start = ((), (), s32[]{:S(2)}) async-start(), calls=%async_computation.3 | async-start | bytes 4300800 | tf_op jit(solution)/shard_map/all_gather | solution.py:51
  57.8 105.1 %all-gather.6.cloned.1.call-start = ((), (), s32[]{:S(2)}) async-start(), calls=%async_computation.2 | async-start | bytes 1966080 | tf_op jit(solution)/shard_map/all_gather | solution.py:54
Sparse Core Ops, SparseCore 0:
  8.9 21.9 all-gather.3
  57.2 66.0 all-reduce.1
  124.9 11.1 all-gather.7
  137.5 25.3 all-gather.5
where the time goes:
time: 176 us; the launch traced here: 175 us
  waiting for transfers between devices  62.4 us (35%)
  local copies, waits for them, and re-layouts  37.3 us (21%)
  blocking collectives  31.6 us (18%)
  matrix products  24.9 us (14%)
  between operations  13.3 us (8%)
  other arithmetic  5.39 us (3%)
    psum x1, blocking collectives, body(): state, ksum = lax.psum((state, ksum), ('seq', 'rep'))  31.6 us
    psum x1, waiting for transfers between devices, body(): state, ksum = lax.psum((state, ksum), ('seq', 'rep'))  30.4 us
    all_gather x1, waiting for transfers between devices, body(): lax.all_gather(attn, 'mp', axis=1, tiled=True)  26.8 us
    dot_general x2, local copies, waits for them, and re-layouts, body(): jnp.einsum('td,dcm->tcm', modulated, lax.all_gather(w_qkv, 'rep', axis=0,...  19.3 us
    dot_general x1, matrix products, body(): jnp.einsum('td,dcm->tcm', modulated, lax.all_gather(w_qkv, 'rep', axis=0,...  8.95 us
    unnamed x16, local copies, waits for them, and re-layouts  7.35 us
    dot_general x1, matrix products, body(): jnp.dot(lax.all_gather(attn, 'mp', axis=1, tiled=True), out_full, preferr...  5.59 us
    dot_general x1, matrix products, body(): own_state = jnp.einsum('si,ihef->shef', picker, state, precision=hi)  3.93 us
  transfers between devices with their start and end apart: 4, of which 4 were waited for; matrix products, arithmetic and copies ran while one was open for 19% of the time, Pallas kernels for 0%

commit v1 on v0

--- a/solution.py
+++ b/solution.py
@@ -5,6 +5,20 @@
 
 D = 2240
 HD = 32
+
+
+def return_all_the_roads(u, dev_axis):
+    view_out, t1 = (jax.lax.axis_size(dev_axis), jax.lax.axis_index(dev_axis))
+    small, v1 = (u, 1)
+    while v1 < view_out:
+        current_block = jax.lax.ppermute(
+            small, dev_axis, list(map(lambda k: (k, k ^ v1), range(view_out)))
+        )
+        vec_out = jnp.concatenate([small, current_block], axis=1)
+        r2 = jnp.concatenate([current_block, small], axis=1)
+        small = jnp.where(t1 & v1 == 0, vec_out, r2)
+        v1 = 2 * v1
+    return small
 
 
 def body(tokens, slot_image, modulation, w_qkv, w_out):
@@ -51,7 +65,7 @@
     out_full = lax.all_gather(w_out, "rep", axis=0, tiled=True)
     cols = out_full.shape[1]
     projected = jnp.dot(
-        lax.all_gather(attn, "mp", axis=1, tiled=True), out_full, preferred_element_type=jnp.float32
+        return_all_the_roads(attn, "mp"), out_full, preferred_element_type=jnp.float32
     )
     offset = lax.axis_index("mp") * cols
     own_tokens = (

time: 176 us -> 158 us (0.90)
  waiting for transfers between devices: 62.4 us -> 44.3 us
    all_gather x1 -> x0, waiting for transfers between devices: 26.8 us -> none  [body(): lax.all_gather(attn, 'mp', axis=1, tiled=True)]
    ppermute x0 -> x1, waiting for transfers between devices: none -> 9.19 us  [return_all_the_roads(): jax.lax.ppermute(small, dev_axis, list(map(lambda k: (k, k ^ v1), range(v...]
  transfers between devices with their start and end apart: 4 -> 4, of which waited for: 4 -> 4; matrix products, arithmetic and copies ran while one was open for 19% -> 21% of each run, Pallas kernels for 0% -> 0%
where the time goes in v1:
time: 158 us; the launch traced here: 157 us
  waiting for transfers between devices  44.3 us (28%)
  local copies, waits for them, and re-layouts  36.4 us (23%)
  blocking collectives  31.4 us (20%)
  matrix products  24.9 us (16%)
  between operations  13.3 us (8%)
  other arithmetic  5.38 us (3%)
  starting transfers between devices  1.62 us (1%)
    psum x1, blocking collectives, body(): state, ksum = lax.psum((state, ksum), ('seq', 'rep'))  31.4 us
    psum x1, waiting for transfers between devices, body(): state, ksum = lax.psum((state, ksum), ('seq', 'rep'))  30.6 us
    dot_general x2, local copies, waits for them, and re-layouts, body(): jnp.einsum('td,dcm->tcm', modulated, lax.all_gather(w_qkv, 'rep', axis=0,...  19.3 us
    ppermute x1, waiting for transfers between devices, return_all_the_roads(): jax.lax.ppermute(small, dev_axis, list(map(lambda k: (k, k ^ v1), range(v...  9.19 us
    dot_general x1, matrix products, body(): jnp.einsum('td,dcm->tcm', modulated, lax.all_gather(w_qkv, 'rep', axis=0,...  8.94 us
    unnamed x16, local copies, waits for them, and re-layouts  6.52 us
    dot_general x1, matrix products, body(): jnp.dot(return_all_the_roads(attn, 'mp'), out_full, preferred_element_typ...  5.61 us
    dot_general x1, matrix products, body(): own_state = jnp.einsum('si,ihef->shef', picker, state, precision=hi)  3.93 us
  transfers between devices with their start and end apart: 4, of which 4 were waited for; matrix products, arithmetic and copies ran while one was open for 21% of the time, Pallas kernels for 0%

profile of v1, /device:TPU:0, one launch (start us, length us, event | category | flops | bytes accessed | tf_op | source)
XLA Modules:
  0.0 157.4 jit_solution(15160977016026077519)
XLA Ops:
  6.5 0.7 all-gather.3.cloned.1.call-update
  8.1 0.4 copy.12
  8.5 2.7 %mul.34 = f32[2,256,2240]{1,0,2:T(2,128)S(1)} broadcast(f32[2,2240]{0,1:T(8,128)S(1)} %copy.12), dimensions={0,2} | broadcast | bytes 4605440 | tf_op jit(solution)/shard_map/mul | solution.py:40
  11.3 2.6 %copy.34 = f32[280,8,2,256]{3,1,2,0:T(8,128)} copy(f32[280,8,2,256]{3,2,1,0:T(2,128)S(1)} %bitcast.79) | data formatting | bytes 9175040
  13.8 0.4 copy.13
  14.2 2.7 %add.57 = f32[2,256,2240]{1,0,2:T(2,128)S(1)} broadcast(f32[2,2240]{0,1:T(8,128)S(1)} %copy.13), dimensions={0,2} | broadcast | bytes 4605440 | tf_op jit(solution)/shard_map/add | solution.py:40
  17.0 0.5 copy.35
  17.5 1.5 copy-done
  19.0 0.4 convert_reduce_fusion
  19.4 0.7 fusion.2
  20.1 3.0 %fusion.5 = bf16[512,2240]{0,1:T(8,128)(2,1)} fusion(f32[512,2240]{0,1:T(8,128)S(1)} %bitcast.78, f32[512,2240]{0,1:T(8,128)S(1)} %bitcast.77, bf16[512,2240]{0,1:T(8,128)(2,1)S(1)} %copy-done, f32[512]{0:T(512)S(1)} %add_sqrt_fusion, f32[512]{0:T(512)S(1)} %broadcast_multiply_fusion), kind=kLoop, calls=%fused_computation.7 | loop fusion | flops 6881280 | bytes 13766656 | tf_op jit(solution)/shard_map/convert_element_type | solution.py:40
  23.1 6.1 %dot_general.43 = bf16[2,256,2240]{1,0,2:T(2,128)(2,1)} reshape(bf16[512,2240]{0,1:T(8,128)(2,1)} %fusion.5) | data formatting | bytes 4587520 | tf_op jit(solution)/shard_map/td,dcm->tcm/dot_general | solution.py:44
  29.1 1.8 %all-gather.3.cloned.1.call-done = bf16[2240,3,640]{2,0,1:T(8,128)(2,1)} async-done(((bf16[1120,3,640]{2,0,1:T(8,128)(2,1)}), bf16[2240,3,640]{2,0,1:T(8,128)(2,1)}) %all-gather.3.cloned.1.call-update) | async-done | bytes 8601616 | tf_op jit(solution)/shard_map/all_gather | solution.py:47
  30.9 13.2 %copy.14 = bf16[3,640,2240]{2,1,0:T(8,128)(2,1)} copy(bf16[3,640,2240]{1,2,0:T(8,128)(2,1)} %bitcast.83) | data formatting | bytes 17203200 | tf_op jit(solution)/shard_map/td,dcm->tcm/dot_general | solution.py:44
  44.1 8.9 %fusion.10 = bf16[2,256,3,20,32]{1,4,3,2,0:T(8,128)(2,1)S(1)} fusion(bf16[3,20,32,2240,1]{3,2,1,0,4:T(8,128)(2,1)} %bitcast.82, bf16[2,256,2240,1,1]{1,0,2,4,3:T(2,128)(2,1)} %bitcast.86), kind=kOutput, calls=%fused_computation.13 | convolution fusion | flops 4404019200 | bytes 12861440 | tf_op jit(solution)/shard_map/td,dcm->tcm/dot_general | solution.py:44
  53.1 0.3 fusion.24
  53.4 1.9 %fusion.28 = f32[6,20,32,32]{3,0,2,1:T(8,128)S(1)} fusion(f32[2,20,32,32]{3,2,1,0:T(8,128)S(1)} %fusion.24, s32[2]{0:T(128)S(1)} %copy-done.3), kind=kOutput, calls=%fused_computation.37 | convolution fusion | flops 2949132 | bytes 655368 | tf_op jit(solution)/shard_map/si,shef->ihef/dot_general | solution.py:56
  55.4 1.7 %copy.20 = f32[6,20,32,32]{3,2,1,0:T(8,128)} copy(f32[6,20,32,32]{3,0,2,1:T(8,128)S(1)} %fusion.28) | data formatting | bytes 983040 | tf_op jit(solution)/shard_map/si,shef->ihef/dot_general | solution.py:56
  57.1 0.7 all-gather.5.cloned.1.call-update
  57.8 1.3 convert_reduce_fusion.1
  59.5 31.4 %psum.15 = f32[6,20,32]{2,1,0:T(8,128)S(1)} all-reduce(f32[6,20,32]{2,1,0:T(8,128)S(1)} %copy.24), channel_id=1, replica_groups=mesh['groups'=2,'seq'=4,'mp'=2,'rep'=2] {'seq','rep'}, use_global_device_ids=true, to_apply=%region_4.5 | all-reduce | flops 3840 | bytes 30720 | tf_op jit(solution)/shard_map/psum | solution.py:58
  91.1 1.5 fusion.33
  92.7 30.6 %all-reduce.2.cloned.1.call-done = f32[6,20,32,32]{3,2,1,0:T(8,128)} async-done(((f32[6,20,32,32]{3,2,1,0:T(8,128)}), f32[6,20,32,32]{3,2,1,0:T(8,128)}) %all-reduce.2.cloned.1.call-update) | async-done | bytes 491536 | tf_op jit(solution)/shard_map/psum | solution.py:58
  123.3 3.9 %fusion.8 = f32[2,20,32,32]{3,0,2,1:T(2,128)S(1)} fusion(f32[6,20,32,32]{3,2,1,0:T(8,128)} %all-reduce.2.cloned.1.call-done, s32[2]{0:T(128)S(1)} %copy-done.3), kind=kOutput, calls=%fused_computation.11 | convolution fusion | flops 2949132 | bytes 655368 | tf_op jit(solution)/shard_map/si,ihef->shef/dot_general | solution.py:59
  127.2 1.9 %fusion.13 = bf16[2,256,20,32]{1,3,2,0:T(8,128)(2,1)S(1)} fusion(f32[2,20,32,32]{3,0,2,1:T(2,128)S(1)} %fusion.8, f32[2,256,20]{1,2,0:T(8,128)S(1)} %fusion.37, bf16[2,256,3,20,32]{1,4,3,2,0:T(8,128)(2,1)} %copy-done.2), kind=kOutput, calls=%fused_computation.17 | convolution fusion | flops 127467520 | bytes 1515520 | tf_op jit(solution)/shard_map/slhe,shef->slhf/dot_general | solution.py:62
  129.1 0.7 copy.16
  129.9 1.5 collective-permute-start
  131.8 1.3 mul.31
  133.1 1.6 %copy.33 = f32[140,8,2,256]{3,1,2,0:T(8,128)} copy(f32[140,8,2,256]{3,2,1,0:T(2,128)S(1)} %bitcast.81) | data formatting | bytes 4587520
  134.7 1.4 all-gather.5.cloned.1.call-done
  136.1 9.2 %collective-permute-done = bf16[512,640]{0,1:T(8,128)(2,1)} collective-permute-done((bf16[512,640]{0,1:T(8,128)(2,1)S(1)}, bf16[512,640]{0,1:T(8,128)(2,1)}, u32[]{:S(2)}, u32[]{:S(2)}) %collective-permute-start) | collective-permute-done | bytes 655392 | tf_op jit(solution)/shard_map/ppermute | solution.py:14
  145.3 5.6 %fusion.7 = bf16[512,1120]{0,1:T(8,128)(2,1)} fusion(f32[512,1120]{0,1:T(8,128)} %bitcast.85, bf16[1280,1120]{0,1:T(8,128)(2,1)} %all-gather.5.cloned.1.call-done, bf16[512,640]{0,1:T(8,128)(2,1)} %collective-permute-done, bf16[512,640]{0,1:T(8,128)(2,1)S(1)} %bitcast.89, pred[]{:T(512)S(6)} %eq.19, bf16[512,2240]{0,1:T(8,128)(2,1)S(1)} %copy-done, ...), kind=kOutput, calls=%fused_computation.10 | convolution fusion | flops 1476198400 | bytes 8765445 | tf_op jit(solution)/shard_map/dot_general | solution.py:67
  (29 shorter events, 1.9 us)
Async XLA Ops:
  6.5 0.9 copy-start.1
  6.5 24.4 %all-gather.3.cloned.1.call-start = ((), (), s32[]{:S(2)}) async-start(), calls=%async_computation | async-start | bytes 12902400 | tf_op jit(solution)/shard_map/all_gather | solution.py:47
  6.5 1.3 copy-start.3
  7.3 116.0 %all-reduce.2.cloned.1.call-start = ((), (), s32[]{:S(2)}) async-start(), calls=%async_computation.1 | async-start | bytes 3932160 | tf_op jit(solution)/shard_map/psum | solution.py:58
  14.2 5.9 %slice-start = ((s8[4587520]{0:T(1024)(128)(4,1)}), s8[4194304]{0:T(1024)(128)(4,1)S(1)}, s32[]{:S(2)}) async-start(s8[4587520]{0:T(1024)(128)(4,1)} %bitcast.75), calls=%async_computation.3 | async-start | bytes 8388608
  17.0 2.1 %copy-start = (bf16[512,2240]{0,1:T(8,128)(2,1)S(1)}, bf16[512,2240]{0,1:T(8,128)(2,1)}, u32[]{:S(2)}) copy-start(bf16[512,2240]{0,1:T(8,128)(2,1)} %param.5) | copy-start | bytes 6881284
  17.0 3.1 %slice-start.1 = ((s8[4587520]{0:T(1024)(128)(4,1)}), s8[393216]{0:T(1024)(128)(4,1)S(1)}, s32[]{:S(2)}) async-start(s8[4587520]{0:T(1024)(128)(4,1)} %bitcast.75), calls=%async_computation.4 | async-start | bytes 786432
  53.1 2.3 %copy-start.2 = (bf16[2,256,3,20,32]{1,4,3,2,0:T(8,128)(2,1)}, bf16[2,256,3,20,32]{1,4,3,2,0:T(8,128)(2,1)S(1)}, u32[]{:S(2)}) copy-start(bf16[2,256,3,20,32]{1,4,3,2,0:T(8,128)(2,1)S(1)} %fusion.10) | copy-start | bytes 5898244
  57.1 79.0 %all-gather.5.cloned.1.call-start = ((), (), s32[]{:S(2)}) async-start(), calls=%async_computation.2 | async-start | bytes 4300800 | tf_op jit(solution)/shard_map/all_gather | solution.py:65
  129.9 15.4 %collective-permute-start = (bf16[512,640]{0,1:T(8,128)(2,1)S(1)}, bf16[512,640]{0,1:T(8,128)(2,1)}, u32[]{:S(2)}, u32[]{:S(2)}) collective-permute-start(bf16[512,640]{0,1:T(8,128)(2,1)S(1)} %bitcast.88), channel_id=1, source_target_pairs={{0,2},{2,0},{1,3},{3,1},{4,6},{6,4},{5,7},{7,5},{8,10},{10,8},{9,1... | collective-permute-start | bytes 1966088 | tf_op jit(solution)/shard_map/ppermute | solution.py:14
Sparse Core Ops, SparseCore 0:
  8.9 21.9 all-gather.2
  57.2 66.0 all-reduce.1
  124.9 11.1 all-gather.4
